TPU v7x, 32 devices: a whole 2x2x4 slice. The times are simulated.
32 devices in a mesh: groups: 2 (over y), depth: 4 (over z), rows: 2 (over x), cols: 2 (over core).
Axes of the slice: x: 2, y: 2, z: 4, core: 2. Of those that a mesh axis runs over, the one named last changes fastest.
Arguments:
- volume: bfloat16 [4, 16, 16, 3072], P('groups', 'depth', 'rows', 'cols'), parts along dimension 0, may hold values from -6 to 6
- grad_out: bfloat16 [4, 16, 16, 3072], P('groups', 'depth', 'rows', 'cols'), parts along dimension 0, may hold values from -6 to 6
- report: bfloat16 [1536], P('groups'), parts along dimension 0, may hold values from -6 to 6
- conv_kernel: bfloat16 [96, 1, 7, 7, 7], replicated, may hold values from -0.3125 to 0.3125
- conv_bias: float32 [96], replicated, may hold values from -4 to 4
- film_weight: bfloat16 [768, 192], replicated, may hold values from -0.21875 to 0.21875
- film_bias: float32 [192], replicated, may hold values from -3 to 3
- in_weight: bfloat16 [96, 384], replicated, may hold values from -0.625 to 0.625
- in_bias: float32 [384], replicated, may hold values from -3 to 3
- out_weight: bfloat16 [384, 96], replicated, may hold values from -0.3125 to 0.3125
Outputs:
- grad_input: bfloat16 [4, 16, 16, 3072], P('groups', 'depth', 'rows', 'cols'), parts along dimension 0
- grad_kernel: float32 [192, 1, 7, 7, 7], P('groups'), parts along dimension 0
- grad_conv_bias: float32 [192], P('groups'), parts along dimension 0
- grad_film: float32 [384], P('groups'), parts along dimension 0
- grad_in_weight: float32 [192, 384], P('groups'), parts along dimension 0
- grad_in_bias: float32 [768], P('groups'), parts along dimension 0
- grad_out_weight: float32 [768, 96], P('groups'), parts along dimension 0
There are 2 independent parts, one for each index of `groups`. A program takes and returns all parts, laid end to end along the dimension named above; an argument that names none is the same for every part. Nothing has to cross between parts.
All inputs are finite; a program needn't handle non-finite values.
Results may differ from a plain program's by a relative error of at most 0.0062.
Values may be sent and summed in bfloat16 or wider, within the bound.
A program may use at most 64 MiB of HBM per device.

v0:
```python
import math
import jax
import jax.numpy as jnp
from jax import lax
from jax.sharding import PartitionSpec as P

K = 7
epsilon = 1e-06
last_dims = ("NDHWC", "OIDHW", "NDHWC")
grad_dims = ("NDHWC", "DHWIO", "NDHWC")


def padded_2(block, sides, width):
    for axis, dim in sides:
        count = lax.axis_size(axis)
        forward = [(i, i + 1) for i in range(count - 1)]
        backward = [(target, source) for source, target in forward]
        low = lax.ppermute(
            lax.slice_in_dim(block, block.shape[dim] - width, None, axis=dim), axis, forward
        )
        high = lax.ppermute(lax.slice_in_dim(block, 0, width, axis=dim), axis, backward)
        block = jnp.concatenate([low, block, high], axis=dim)
    return block


def depthwise(padded, kernel):
    return lax.conv_general_dilated(
        padded,
        kernel,
        (1, 1, 1),
        "VALID",
        dimension_numbers=last_dims,
        feature_group_count=kernel.shape[0],
        preferred_element_type=jnp.float32,
    )


def widen(field):
    half_width = K // 2
    result = padded_2(field, (("depth", 1), ("rows", 2), ("cols", 3)), half_width)
    return result


def pointwise(conv_flat, grad_flat, film_vec, in_weight, in_bias, out_weight):
    channels = conv_flat.shape[0]
    chan_mean = jnp.mean(conv_flat, axis=0)
    centred = conv_flat - chan_mean
    variance = jnp.mean(centred * centred, axis=0)
    inverse = lax.rsqrt(variance + epsilon)
    normed = centred * inverse
    scale_vec = 1.0 + film_vec[:channels, None]
    hidden_in = (normed * scale_vec + film_vec[channels:, None]).astype(jnp.bfloat16)
    pre_act = jnp.dot(in_weight.T, hidden_in, preferred_element_type=jnp.float32) + in_bias[:, None]
    post_act, gelu_back = jax.vjp(jax.nn.gelu, pre_act)
    act_low = post_act.astype(jnp.bfloat16)
    grad_act = jnp.dot(out_weight, grad_flat, preferred_element_type=jnp.float32)
    grad_pre = gelu_back(grad_act)[0]
    grad_low = grad_pre.astype(jnp.bfloat16)
    grad_hidden = jnp.dot(in_weight, grad_low, preferred_element_type=jnp.float32)
    grad_out_w = jnp.dot(act_low, grad_flat.T, preferred_element_type=jnp.float32)
    grad_in_w = jnp.dot(hidden_in, grad_low.T, preferred_element_type=jnp.float32)
    grad_in_b = jnp.sum(grad_pre, axis=1)
    grad_film = jnp.concatenate(
        [jnp.sum(grad_hidden * normed, axis=1), jnp.sum(grad_hidden, axis=1)]
    )
    grad_normed = grad_hidden * scale_vec
    slope = (
        (
            grad_normed
            - jnp.mean(grad_normed, axis=0)
            - normed * jnp.mean(grad_normed * normed, axis=0)
        )
        * inverse
    ).astype(jnp.bfloat16)
    return (slope, (grad_in_w, grad_in_b, grad_out_w, grad_film))


def local(
    volume,
    grad_out,
    report,
    conv_kernel,
    conv_bias,
    film_weight,
    film_bias,
    in_weight,
    in_bias,
    out_weight,
):
    crops, slices, lines, merged = volume.shape
    channels = conv_kernel.shape[0]
    local_shape = (crops, slices, lines, merged // channels, channels)
    film_vec = (
        jnp.dot(report[None, :], film_weight, preferred_element_type=jnp.float32)[0] + film_bias
    )
    local_vol = volume.reshape(local_shape)
    local_grad = grad_out.reshape(local_shape)
    padded = widen(local_vol)
    conv_out = depthwise(padded, conv_kernel) + conv_bias
    conv_flat = conv_out.reshape(-1, channels).T
    grad_flat = local_grad.reshape(-1, channels).T
    slope_flat, local_grads = pointwise(
        conv_flat, grad_flat, film_vec, in_weight, in_bias, out_weight
    )
    voxel_count = (
        conv_flat.shape[1] * lax.axis_size("depth") * lax.axis_size("rows") * lax.axis_size("cols")
    )
    factor = 1.0 / math.sqrt(voxel_count)
    term_in_w = local_grads[0] * factor
    term_in_b = local_grads[1] * factor
    term_out_w = local_grads[2] * factor
    term_film = local_grads[3] * factor
    summed_mlp = lax.psum((term_in_w, term_in_b, term_out_w, term_film), ("depth", "rows", "cols"))
    slope_vol = slope_flat.T.reshape(local_shape)
    slope_pad = widen(slope_vol)
    flipped = conv_kernel[:, :, ::-1, ::-1, ::-1]
    grad_input = (
        (local_grad.astype(jnp.float32) + depthwise(slope_pad, flipped))
        .astype(jnp.bfloat16)
        .reshape(volume.shape)
    )
    kernel_local = jnp.zeros((1, K, K, K, channels), jnp.float32)
    for crop_index in range(crops):
        kernel_local = kernel_local + lax.conv_general_dilated(
            padded[crop_index][None],
            slope_vol[crop_index][:, :, :, None, :],
            (1, 1, 1),
            "VALID",
            dimension_numbers=grad_dims,
            feature_group_count=channels,
            preferred_element_type=jnp.float32,
        )
    term_kernel = jnp.moveaxis(kernel_local[0], 3, 0)[:, None] * factor
    term_bias = jnp.sum(slope_flat.astype(jnp.float32), axis=1) * factor
    summed_conv = lax.psum((term_kernel, term_bias), ("depth", "rows", "cols"))
    totals = tuple(summed_mlp) + tuple(summed_conv)
    return (grad_input, totals[4], totals[5], totals[3], totals[0], totals[1], totals[2])


def solution(mesh):
    in_specs = (
        P("groups", "depth", "rows", "cols"),
        P("groups", "depth", "rows", "cols"),
        P("groups"),
        P(),
        P(),
        P(),
        P(),
        P(),
        P(),
        P(),
    )
    out_specs = (
        P("groups", "depth", "rows", "cols"),
        P("groups", None, None, None, None),
        P("groups"),
        P("groups"),
        P("groups", None),
        P("groups"),
        P("groups", None),
    )
    return jax.shard_map(local, mesh=mesh, in_specs=in_specs, out_specs=out_specs, check_vma=False)
```

profile of v0, /device:TPU:8, one launch (start us, length us, event | category | flops | bytes accessed | tf_op | source)
XLA Modules:
  0.0 245.4 jit_solution(1171630249008193471)
XLA Ops:
  8.8 3.5 %collective-permute-start = (bf16[2,3,8,16,96]{4,0,3,2,1:T(2,128)(2,1)S(1)}, bf16[2,3,8,16,96]{4,0,3,2,1:T(2,128)(2,1)S(1)}, u32[]{:S(2)}, u32[]{:S(2)}) collective-permute-start(bf16[2,3,8,16,96]{4,0,3,2,1:T(2,128)(2,1)S(1)} %copy.119), channel_id=1, source_target_pairs={{0,4},{4,8},{8,12},{1,5},{5,9},{9,13},{2,6},{6,10},{10,14},{3,7},{... | collective-permute-start | bytes 442376 | tf_op jit(solution)/shard_map/ppermute | solution.py:18
  12.5 2.4 collective-permute-start.1
  15.3 2.0 collective-permute-done
  17.7 3.0 %collective-permute-done.1 = bf16[2,3,8,16,96]{4,0,3,2,1:T(2,128)(2,1)S(1)} collective-permute-done((bf16[2,3,8,16,96]{4,0,3,2,1:T(2,128)(2,1)S(1)}, bf16[2,3,8,16,96]{4,0,3,2,1:T(2,128)(2,1)S(1)}, u32[]{:S(2)}, u32[]{:S(2)}) %collective-permute-start.1) | collective-permute-done | bytes 147488 | tf_op jit(solution)/shard_map/ppermute | solution.py:21
  21.2 3.4 %collective-permute-start.2 = (bf16[2,10,3,16,96]{4,0,3,2,1:T(2,128)(2,1)S(1)}, bf16[2,10,3,16,96]{4,0,3,2,1:T(2,128)(2,1)S(1)}, u32[]{:S(2)}, u32[]{:S(2)}) collective-permute-start(bf16[2,10,3,16,96]{4,0,3,2,1:T(2,128)(2,1)S(1)} %get-tuple-element.57), channel_id=1, source_target_pairs={{0,2},{1,3},{4,6},{5,7},{8,10},{9,11},{12,14},{13,15},{16,18},{17,... | collective-permute-start | bytes 552968 | tf_op jit(solution)/shard_map/ppermute | solution.py:18
  26.1 2.6 %collective-permute-done.2 = bf16[2,10,3,16,96]{4,0,3,2,1:T(2,128)(2,1)S(1)} collective-permute-done((bf16[2,10,3,16,96]{4,0,3,2,1:T(2,128)(2,1)S(1)}, bf16[2,10,3,16,96]{4,0,3,2,1:T(2,128)(2,1)S(1)}, u32[]{:S(2)}, u32[]{:S(2)}) %collective-permute-start.2) | collective-permute-done | bytes 184352 | tf_op jit(solution)/shard_map/ppermute | solution.py:18
  28.7 4.1 %collective-permute-done.3 = bf16[2,10,3,16,96]{4,0,3,2,1:T(2,128)(2,1)S(1)} collective-permute-done((bf16[2,10,3,16,96]{4,0,3,2,1:T(2,128)(2,1)S(1)}, bf16[2,10,3,16,96]{4,0,3,2,1:T(2,128)(2,1)S(1)}, u32[]{:S(2)}, u32[]{:S(2)}) %collective-permute-start.3) | collective-permute-done | bytes 184352 | tf_op jit(solution)/shard_map/ppermute | solution.py:21
  34.9 1.5 collective-permute-start.5
  36.5 1.8 collective-permute-done.5
  38.2 7.8 %pad_maximum_fusion = bf16[2,10,14,22,96]{4,0,3,2,1:T(2,128)(2,1)S(1)} fusion(bf16[2,10,14,3,96]{4,0,3,2,1:T(2,128)(2,1)S(1)} %collective-permute-done.5, bf16[2,10,3,16,96]{4,0,3,2,1:T(2,128)(2,1)S(1)} %collective-permute-done.3, bf16[2,10,8,16,96]{4,0,3,2,1:T(2,128)(2,1)S(1)} %constant_dynamic-update-slice_fusion, ...), kind=kLoop, calls=%fused_computation.6 | loop fusion | flops 2365440 | bytes 2365440 | tf_op jit(solution)/shard_map/concatenate | solution.py:22
  46.0 19.1 %fusion.59 = (f32[2,4,8,16]{0,3,2,1:T(8,128)S(1)}, f32[2,4,8,16,96]{4,0,3,2,1:T(2,128)S(1)}) fusion(f32[96]{0:T(128)S(1)} %copy-done.13, bf16[2,10,14,22,96]{4,0,3,2,1:T(2,128)(2,1)S(1)} %pad_maximum_fusion, bf16[96,1,7,7,7]{0,4,3,2,1:T(8,128)(2,1)S(1)} %copy-done.10), kind=kOutput, calls=%fused_computation.92 | convolution fusion | flops 67632128 | bytes 1646272 | tf_op jit(solution)/shard_map/conv_general_dilated | solution.py:27
  66.5 1.3 convolution_multiply_fusion.1
  70.1 15.6 %fusion = f32[1,7,7,7,96]{4,0,3,2,1:T(1,128)S(1)} fusion(bf16[2,10,14,22,96]{4,0,3,2,1:T(2,128)(2,1)} %copy-done.1, bf16[4,8,16,1,96]{4,2,1,0,3:T(8,128)(2,1)S(1)} %bitcast.90), kind=kOutput, calls=%fused_computation.2 | convolution fusion | flops 33718272 | bytes 1412736 | tf_op jit(solution)/shard_map/conv_general_dilated | solution.py:124
  86.0 3.6 %collective-permute-start.6 = (bf16[2,3,8,16,96]{4,0,3,2,1:T(2,128)(2,1)S(1)}, bf16[2,3,8,16,96]{4,0,3,2,1:T(2,128)(2,1)S(1)}, u32[]{:S(2)}, u32[]{:S(2)}) collective-permute-start(bf16[2,3,8,16,96]{4,0,3,2,1:T(2,128)(2,1)S(1)} %copy.121), channel_id=1, source_target_pairs={{0,4},{4,8},{8,12},{1,5},{5,9},{9,13},{2,6},{6,10},{10,14},{3,7},{... | collective-permute-start | bytes 442376 | tf_op jit(solution)/shard_map/ppermute | solution.py:18
  89.9 2.4 collective-permute-start.7
  92.3 13.7 %fusion.26 = f32[1,7,7,7,96]{4,0,3,2,1:T(1,128)S(1)} fusion(f32[1,7,7,7,96]{4,0,3,2,1:T(1,128)S(1)} %fusion, bf16[2,10,14,22,96]{4,0,3,2,1:T(2,128)(2,1)S(1)} %copy-done.2, bf16[4,8,16,1,96]{4,2,1,0,3:T(8,128)(2,1)S(1)} %bitcast.89), kind=kOutput, calls=%fused_computation.33 | convolution fusion | flops 33784128 | bytes 1544448 | tf_op jit(solution)/shard_map/conv_general_dilated | solution.py:124
  108.0 1.5 collective-permute-start.8
  111.8 2.8 %collective-permute-done.8 = bf16[2,10,3,16,96]{4,0,3,2,1:T(2,128)(2,1)S(1)} collective-permute-done((bf16[2,10,3,16,96]{4,0,3,2,1:T(2,128)(2,1)S(1)}, bf16[2,10,3,16,96]{4,0,3,2,1:T(2,128)(2,1)S(1)}, u32[]{:S(2)}, u32[]{:S(2)}) %collective-permute-start.8) | collective-permute-done | bytes 184352 | tf_op jit(solution)/shard_map/ppermute | solution.py:18
  114.5 4.1 %collective-permute-done.9 = bf16[2,10,3,16,96]{4,0,3,2,1:T(2,128)(2,1)S(1)} collective-permute-done((bf16[2,10,3,16,96]{4,0,3,2,1:T(2,128)(2,1)S(1)}, bf16[2,10,3,16,96]{4,0,3,2,1:T(2,128)(2,1)S(1)}, u32[]{:S(2)}, u32[]{:S(2)}) %collective-permute-start.9) | collective-permute-done | bytes 184352 | tf_op jit(solution)/shard_map/ppermute | solution.py:21
  122.1 24.1 %all-reduce = (f32[96]{0:T(128)}, f32[192]{0:T(256)}, f32[384]{0:T(512)}) all-reduce(f32[96]{0:T(128)S(1)} %broadcast_multiply_fusion.4, f32[192]{0:T(256)S(1)} %maximum_multiply_fusion, f32[384]{0:T(512)S(1)} %broadcast_multiply_fusion.3), channel_id=1, replica_groups=mesh['groups'=2,'depth'=4,'rows'=2,'cols'=2] {'depth','rows','cols'}, use_global_device_ids=true, to_apply=%region_6.0 | all-reduce | flops 672 | bytes 5376 | tf_op jit(solution)/shard_map/psum | solution.py:135
  146.2 59.3 %all-reduce.4.cloned.1.call-done = (f32[96,1,7,7,7]{0,4,3,2,1:T(8,128)}, f32[96,384]{1,0:T(8,128)}, f32[384,96]{0,1:T(8,128)}) async-done(((f32[96,1,7,7,7]{0,4,3,2,1:T(8,128)}, f32[96,384]{1,0:T(8,128)}, f32[384,96]{0,1:T(8,128)}), (f32[96,1,7,7,7]{0,4,3,2,1:T(8,128)}, f32[96,384]{1,0:T(8,128)}, f32[384,96]{0,1:T(8,128)})) %all-reduce.4.cloned.1.call-update) | async-done | bytes 426640 | tf_op jit(solution)/shard_map/psum | solution.py:135
  205.5 1.8 copy.102
  207.3 7.8 %fusion.81 = bf16[2,10,14,22,96]{4,0,3,2,1:T(2,128)(2,1)S(1)} fusion(bf16[2,10,14,3,96]{4,0,3,2,1:T(2,128)(2,1)S(1)} %collective-permute-done.11, bf16[2,10,3,16,96]{4,0,3,2,1:T(2,128)(2,1)S(1)} %collective-permute-done.9, bf16[2,10,8,16,96]{4,0,3,2,1:T(2,128)(2,1)S(1)} %constant_dynamic-update-slice_fusion.3, ...), kind=kLoop, calls=%fused_computation.8.clone.1 | loop fusion | flops 2365440 | bytes 2365440 | tf_op jit(solution)/shard_map/conv_general_dilated | solution.py:27
  215.1 20.6 %fusion.4 = f32[2,4,8,16,96]{4,0,3,2,1:T(2,128)S(1)} fusion(bf16[96,1,7,7,7]{0,4,3,2,1:T(8,128)(2,1)S(1)} %copy-done.11, bf16[2,10,14,22,96]{4,0,3,2,1:T(2,128)(2,1)S(1)} %fusion.81), kind=kOutput, calls=%fused_computation.7 | convolution fusion | flops 67436544 | bytes 1641792 | tf_op jit(solution)/shard_map/conv_general_dilated | solution.py:27
  (89 shorter events, 20.7 us)
Async XLA Ops:
  7.2 18.8 %copy-start = (bf16[768,192]{0,1:T(8,128)(2,1)S(1)}, bf16[768,192]{0,1:T(8,128)(2,1)}, u32[]{:S(2)}) copy-start(bf16[768,192]{0,1:T(8,128)(2,1)} %param.15) | copy-start | bytes 884740
  7.2 7.6 %copy-start.3 = (bf16[2,4,8,1536]{3,2,1,0:T(8,128)(2,1)S(1)}, bf16[2,4,8,1536]{3,2,1,0:T(8,128)(2,1)}, u32[]{:S(2)}) copy-start(bf16[2,4,8,1536]{3,2,1,0:T(8,128)(2,1)} %param.11) | copy-start | bytes 589828
  7.2 8.1 %copy-start.7 = (bf16[768]{0:T(1024)(128)(2,1)S(1)}, bf16[768]{0:T(1024)(128)(2,1)}, u32[]{:S(2)}) copy-start(bf16[768]{0:T(1024)(128)(2,1)} %param.12) | copy-start | bytes 4612
  7.2 198.3 %all-reduce.4.cloned.1.call-start = ((), (), s32[]{:S(2)}) async-start(), calls=%async_computation | async-start | bytes 991232 | tf_op jit(solution)/shard_map/psum | solution.py:135
  8.8 8.5 %collective-permute-start = (bf16[2,3,8,16,96]{4,0,3,2,1:T(2,128)(2,1)S(1)}, bf16[2,3,8,16,96]{4,0,3,2,1:T(2,128)(2,1)S(1)}, u32[]{:S(2)}, u32[]{:S(2)}) collective-permute-start(bf16[2,3,8,16,96]{4,0,3,2,1:T(2,128)(2,1)S(1)} %copy.119), channel_id=1, source_target_pairs={{0,4},{4,8},{8,12},{1,5},{5,9},{9,13},{2,6},{6,10},{10,14},{3,7},{... | collective-permute-start | bytes 442376 | tf_op jit(solution)/shard_map/ppermute | solution.py:18
  12.5 8.3 %collective-permute-start.1 = (bf16[2,3,8,16,96]{4,0,3,2,1:T(2,128)(2,1)S(1)}, bf16[2,3,8,16,96]{4,0,3,2,1:T(2,128)(2,1)S(1)}, u32[]{:S(2)}, u32[]{:S(2)}) collective-permute-start(bf16[2,3,8,16,96]{4,0,3,2,1:T(2,128)(2,1)S(1)} %copy.120), channel_id=1, source_target_pairs={{4,0},{8,4},{12,8},{5,1},{9,5},{13,9},{6,2},{10,6},{14,10},{7,3},{... | collective-permute-start | bytes 442376 | tf_op jit(solution)/shard_map/ppermute | solution.py:21
  15.1 11.0 %copy-start.9 = (f32[192]{0:T(256)S(1)}, f32[192]{0:T(256)}, u32[]{:S(2)}) copy-start(f32[192]{0:T(256)} %param.16) | copy-start | bytes 2308
  21.2 7.5 %collective-permute-start.2 = (bf16[2,10,3,16,96]{4,0,3,2,1:T(2,128)(2,1)S(1)}, bf16[2,10,3,16,96]{4,0,3,2,1:T(2,128)(2,1)S(1)}, u32[]{:S(2)}, u32[]{:S(2)}) collective-permute-start(bf16[2,10,3,16,96]{4,0,3,2,1:T(2,128)(2,1)S(1)} %get-tuple-element.57), channel_id=1, source_target_pairs={{0,2},{1,3},{4,6},{5,7},{8,10},{9,11},{12,14},{13,15},{16,18},{17,... | collective-permute-start | bytes 552968 | tf_op jit(solution)/shard_map/ppermute | solution.py:18
  24.7 8.2 %collective-permute-start.3 = (bf16[2,10,3,16,96]{4,0,3,2,1:T(2,128)(2,1)S(1)}, bf16[2,10,3,16,96]{4,0,3,2,1:T(2,128)(2,1)S(1)}, u32[]{:S(2)}, u32[]{:S(2)}) collective-permute-start(bf16[2,10,3,16,96]{4,0,3,2,1:T(2,128)(2,1)S(1)} %get-tuple-element.58), channel_id=1, source_target_pairs={{2,0},{3,1},{6,4},{7,5},{10,8},{11,9},{14,12},{15,13},{18,16},{19,... | collective-permute-start | bytes 552968 | tf_op jit(solution)/shard_map/ppermute | solution.py:21
  33.5 2.9 %collective-permute-start.4 = (bf16[2,10,14,3,96]{4,0,3,2,1:T(2,128)(2,1)S(1)}, bf16[2,10,14,3,96]{4,0,3,2,1:T(2,128)(2,1)S(1)}, u32[]{:S(2)}, u32[]{:S(2)}) collective-permute-start(bf16[2,10,14,3,96]{4,0,3,2,1:T(2,128)(2,1)S(1)} %get-tuple-element.53), channel_id=1, source_target_pairs={{0,1},{2,3},{4,5},{6,7},{8,9},{10,11},{12,13},{14,15},{16,17},{18,... | collective-permute-start | bytes 483848 | tf_op jit(solution)/shard_map/ppermute | solution.py:18
  34.9 3.4 %collective-permute-start.5 = (bf16[2,10,14,3,96]{4,0,3,2,1:T(2,128)(2,1)S(1)}, bf16[2,10,14,3,96]{4,0,3,2,1:T(2,128)(2,1)S(1)}, u32[]{:S(2)}, u32[]{:S(2)}) collective-permute-start(bf16[2,10,14,3,96]{4,0,3,2,1:T(2,128)(2,1)S(1)} %get-tuple-element.54), channel_id=1, source_target_pairs={{1,0},{3,2},{5,4},{7,6},{9,8},{11,10},{13,12},{15,14},{17,16},{19,... | collective-permute-start | bytes 483848 | tf_op jit(solution)/shard_map/ppermute | solution.py:21
  36.4 9.5 %copy-start.10 = (bf16[96,1,7,7,7]{0,4,3,2,1:T(8,128)(2,1)S(1)}, bf16[96,1,7,7,7]{0,4,3,2,1:T(8,128)(2,1)}, u32[]{:S(2)}) copy-start(bf16[96,1,7,7,7]{0,4,3,2,1:T(8,128)(2,1)} %param.13) | copy-start | bytes 197572
  36.5 9.6 %copy-start.13 = (f32[96]{0:T(128)S(1)}, f32[96]{0:T(128)}, u32[]{:S(2)}) copy-start(f32[96]{0:T(128)} %param.14) | copy-start | bytes 1156
  46.0 19.1 %copy-start.1 = (bf16[2,10,14,22,96]{4,0,3,2,1:T(2,128)(2,1)}, bf16[2,10,14,22,96]{4,0,3,2,1:T(2,128)(2,1)S(1)}, u32[]{:S(2)}) copy-start(bf16[2,10,14,22,96]{4,0,3,2,1:T(2,128)(2,1)S(1)} %pad_maximum_fusion) | copy-start | bytes 3548164
  66.5 1.4 copy-start.12
  85.8 6.5 %copy-start.2 = (bf16[2,10,14,22,96]{4,0,3,2,1:T(2,128)(2,1)S(1)}, bf16[2,10,14,22,96]{4,0,3,2,1:T(2,128)(2,1)}, u32[]{:S(2)}) copy-start(bf16[2,10,14,22,96]{4,0,3,2,1:T(2,128)(2,1)} %copy-done.1) | copy-start | bytes 3548164
  86.0 21.0 %collective-permute-start.6 = (bf16[2,3,8,16,96]{4,0,3,2,1:T(2,128)(2,1)S(1)}, bf16[2,3,8,16,96]{4,0,3,2,1:T(2,128)(2,1)S(1)}, u32[]{:S(2)}, u32[]{:S(2)}) collective-permute-start(bf16[2,3,8,16,96]{4,0,3,2,1:T(2,128)(2,1)S(1)} %copy.121), channel_id=1, source_target_pairs={{0,4},{4,8},{8,12},{1,5},{5,9},{9,13},{2,6},{6,10},{10,14},{3,7},{... | collective-permute-start | bytes 442376 | tf_op jit(solution)/shard_map/ppermute | solution.py:18
  89.9 17.6 %collective-permute-start.7 = (bf16[2,3,8,16,96]{4,0,3,2,1:T(2,128)(2,1)S(1)}, bf16[2,3,8,16,96]{4,0,3,2,1:T(2,128)(2,1)S(1)}, u32[]{:S(2)}, u32[]{:S(2)}) collective-permute-start(bf16[2,3,8,16,96]{4,0,3,2,1:T(2,128)(2,1)S(1)} %copy.122), channel_id=1, source_target_pairs={{4,0},{8,4},{12,8},{5,1},{9,5},{13,9},{6,2},{10,6},{14,10},{7,3},{... | collective-permute-start | bytes 442376 | tf_op jit(solution)/shard_map/ppermute | solution.py:21
  108.0 6.5 %collective-permute-start.8 = (bf16[2,10,3,16,96]{4,0,3,2,1:T(2,128)(2,1)S(1)}, bf16[2,10,3,16,96]{4,0,3,2,1:T(2,128)(2,1)S(1)}, u32[]{:S(2)}, u32[]{:S(2)}) collective-permute-start(bf16[2,10,3,16,96]{4,0,3,2,1:T(2,128)(2,1)S(1)} %get-tuple-element.55), channel_id=1, source_target_pairs={{0,2},{1,3},{4,6},{5,7},{8,10},{9,11},{12,14},{13,15},{16,18},{17,... | collective-permute-start | bytes 552968 | tf_op jit(solution)/shard_map/ppermute | solution.py:18
  109.5 9.2 %collective-permute-start.9 = (bf16[2,10,3,16,96]{4,0,3,2,1:T(2,128)(2,1)S(1)}, bf16[2,10,3,16,96]{4,0,3,2,1:T(2,128)(2,1)S(1)}, u32[]{:S(2)}, u32[]{:S(2)}) collective-permute-start(bf16[2,10,3,16,96]{4,0,3,2,1:T(2,128)(2,1)S(1)} %get-tuple-element.56), channel_id=1, source_target_pairs={{2,0},{3,1},{6,4},{7,5},{10,8},{11,9},{14,12},{15,13},{18,16},{19,... | collective-permute-start | bytes 552968 | tf_op jit(solution)/shard_map/ppermute | solution.py:21
  119.4 87.9 %collective-permute-start.10 = (bf16[2,10,14,3,96]{4,0,3,2,1:T(2,128)(2,1)S(1)}, bf16[2,10,14,3,96]{4,0,3,2,1:T(2,128)(2,1)S(1)}, u32[]{:S(2)}, u32[]{:S(2)}) collective-permute-start(bf16[2,10,14,3,96]{4,0,3,2,1:T(2,128)(2,1)S(1)} %get-tuple-element.51), channel_id=1, source_target_pairs={{0,1},{2,3},{4,5},{6,7},{8,9},{10,11},{12,13},{14,15},{16,17},{18,... | collective-permute-start | bytes 483848 | tf_op jit(solution)/shard_map/ppermute | solution.py:18
  120.7 86.6 %collective-permute-start.11 = (bf16[2,10,14,3,96]{4,0,3,2,1:T(2,128)(2,1)S(1)}, bf16[2,10,14,3,96]{4,0,3,2,1:T(2,128)(2,1)S(1)}, u32[]{:S(2)}, u32[]{:S(2)}) collective-permute-start(bf16[2,10,14,3,96]{4,0,3,2,1:T(2,128)(2,1)S(1)} %get-tuple-element.52), channel_id=1, source_target_pairs={{1,0},{3,2},{5,4},{7,6},{9,8},{11,10},{13,12},{15,14},{17,16},{19,... | collective-permute-start | bytes 483848 | tf_op jit(solution)/shard_map/ppermute | solution.py:21
  207.3 7.8 %copy-start.11 = (bf16[96,1,7,7,7]{0,4,3,2,1:T(8,128)(2,1)S(1)}, bf16[96,1,7,7,7]{0,4,3,2,1:T(8,128)(2,1)}, u32[]{:S(2)}) copy-start(bf16[96,1,7,7,7]{0,4,3,2,1:T(8,128)(2,1)} %param.13) | copy-start | bytes 197572
  235.8 1.7 copy-start.5
  (3 other events, 2.8 us)
Sparse Core Ops, SparseCore 0:
  111.7 93.8 all-reduce.3
where the time goes:
time: 249 us; the launch traced here: 245 us
  waiting for transfers between devices  79.6 us (32%)
  matrix products  73.7 us (30%)
  starting transfers between devices  24.7 us (10%)
  blocking collectives  24.1 us (10%)
  other arithmetic  17.7 us (7%)
  between operations  15 us (6%)
  local copies, waits for them, and re-layouts  10.4 us (4%)
    psum x1, waiting for transfers between devices, local(): summed_conv = lax.psum((term_kernel, term_bias), ('depth', 'rows', 'cols'))  59.3 us
    conv_general_dilated x2, matrix products, depthwise(): lax.conv_general_dilated(padded, kernel, (1, 1, 1), 'VALID', dimension_nu...  39.7 us
    conv_general_dilated x2, matrix products, local(): lax.conv_general_dilated(padded[crop_index][None], slope_vol[crop_index][...  29.3 us
    psum x1, blocking collectives, local(): summed_conv = lax.psum((term_kernel, term_bias), ('depth', 'rows', 'cols'))  24.1 us
    ppermute x6, starting transfers between devices, padded_2(): lax.ppermute(lax.slice_in_dim(block, block.shape[dim] - width, None, axis...  14.6 us
    ppermute x6, waiting for transfers between devices, padded_2(): lax.ppermute(lax.slice_in_dim(block, 0, width, axis=dim), axis, backward)  13 us
    ppermute x6, starting transfers between devices, padded_2(): lax.ppermute(lax.slice_in_dim(block, 0, width, axis=dim), axis, backward)  10.1 us
    conv_general_dilated x1, other arithmetic, depthwise(): lax.conv_general_dilated(padded, kernel, (1, 1, 1), 'VALID', dimension_nu...  7.79 us
  transfers between devices with their start and end apart: 13, of which 8 were waited for; matrix products, arithmetic and copies ran while one was open for 8% of the time, Pallas kernels for 0%

commit v1 on v0

--- a/solution.py
+++ b/solution.py
@@ -132,7 +132,7 @@
         )
     term_kernel = jnp.moveaxis(kernel_local[0], 3, 0)[:, None] * factor
     term_bias = jnp.sum(slope_flat.astype(jnp.float32), axis=1) * factor
-    summed_conv = lax.psum((term_kernel, term_bias), ("depth", "rows", "cols"))
+    summed_conv = lax.psum(lax.psum((term_kernel, term_bias), ("rows", "cols")), "depth")
     totals = tuple(summed_mlp) + tuple(summed_conv)
     return (grad_input, totals[4], totals[5], totals[3], totals[0], totals[1], totals[2])
 

time: 249 us -> 298 us (1.20)
  waiting for transfers between devices: 79.6 us -> 101 us
  blocking collectives: 24.1 us -> 41.9 us
  local copies, waits for them, and re-layouts: 10.4 us -> 14.7 us
    psum x1 -> x3, waiting for transfers between devices: 59.3 us -> 87.2 us  [the longest x1 56 us: local(): lax.psum((term_in_w, term_in_b, term_out_w, term_film), ('depth', 'rows',...]
    psum x1 -> x3, blocking collectives: 24.1 us -> 41.9 us  [the longest x1 25 us: local(): lax.psum((term_in_w, term_in_b, term_out_w, term_film), ('depth', 'rows',...]
    ppermute x6, waiting for transfers between devices: 13 us -> 8.85 us  [padded_2(): lax.ppermute(lax.slice_in_dim(block, 0, width, axis=dim), axis, backward)]
    unnamed x41 -> x39, local copies, waits for them, and re-layouts: 5.73 us -> 8.5 us
  transfers between devices with their start and end apart: 13 -> 15, of which waited for: 8 -> 7; matrix products, arithmetic and copies ran while one was open for 8% -> 18% of each run, Pallas kernels for 0% -> 0%
where the time goes in v1:
time: 298 us; the launch traced here: 292 us
  waiting for transfers between devices  101 us (34%)
  matrix products  76.5 us (26%)
  blocking collectives  41.9 us (14%)
  starting transfers between devices  26.3 us (9%)
  other arithmetic  17.7 us (6%)
  local copies, waits for them, and re-layouts  14.7 us (5%)
  between operations  14.5 us (5%)
    psum x1, waiting for transfers between devices, local(): lax.psum((term_in_w, term_in_b, term_out_w, term_film), ('depth', 'rows',...  56 us
    conv_general_dilated x2, matrix products, depthwise(): lax.conv_general_dilated(padded, kernel, (1, 1, 1), 'VALID', dimension_nu...  40.2 us
    conv_general_dilated x2, matrix products, local(): lax.conv_general_dilated(padded[crop_index][None], slope_vol[crop_index][...  31.6 us
    psum x1, waiting for transfers between devices, local(): lax.psum((term_kernel, term_bias), ('rows', 'cols'))  31.3 us
    psum x1, blocking collectives, local(): lax.psum((term_in_w, term_in_b, term_out_w, term_film), ('depth', 'rows',...  25 us
    ppermute x6, starting transfers between devices, padded_2(): lax.ppermute(lax.slice_in_dim(block, block.shape[dim] - width, None, axis...  15.4 us
    ppermute x6, starting transfers between devices, padded_2(): lax.ppermute(lax.slice_in_dim(block, 0, width, axis=dim), axis, backward)  10.8 us
    psum x1, blocking collectives, local(): lax.psum(lax.psum((term_kernel, term_bias), ('rows', 'cols')), 'depth')  9.43 us
  transfers between devices with their start and end apart: 15, of which 7 were waited for; matrix products, arithmetic and copies ran while one was open for 18% of the time, Pallas kernels for 0%

profile of v1, /device:TPU:8, one launch (start us, length us, event | category | flops | bytes accessed | tf_op | source)
XLA Modules:
  0.0 292.4 jit_solution(16986937348938562531)
XLA Ops:
  8.7 3.5 %collective-permute-start = (bf16[2,3,8,16,96]{4,0,3,2,1:T(2,128)(2,1)S(1)}, bf16[2,3,8,16,96]{4,0,3,2,1:T(2,128)(2,1)S(1)}, u32[]{:S(2)}, u32[]{:S(2)}) collective-permute-start(bf16[2,3,8,16,96]{4,0,3,2,1:T(2,128)(2,1)S(1)} %copy.119), channel_id=1, source_target_pairs={{0,4},{4,8},{8,12},{1,5},{5,9},{9,13},{2,6},{6,10},{10,14},{3,7},{... | collective-permute-start | bytes 442376 | tf_op jit(solution)/shard_map/ppermute | solution.py:18
  12.5 2.4 collective-permute-start.1
  15.3 2.0 collective-permute-done
  17.7 3.0 %collective-permute-done.1 = bf16[2,3,8,16,96]{4,0,3,2,1:T(2,128)(2,1)S(1)} collective-permute-done((bf16[2,3,8,16,96]{4,0,3,2,1:T(2,128)(2,1)S(1)}, bf16[2,3,8,16,96]{4,0,3,2,1:T(2,128)(2,1)S(1)}, u32[]{:S(2)}, u32[]{:S(2)}) %collective-permute-start.1) | collective-permute-done | bytes 147488 | tf_op jit(solution)/shard_map/ppermute | solution.py:21
  21.2 3.4 %collective-permute-start.2 = (bf16[2,10,3,16,96]{4,0,3,2,1:T(2,128)(2,1)S(1)}, bf16[2,10,3,16,96]{4,0,3,2,1:T(2,128)(2,1)S(1)}, u32[]{:S(2)}, u32[]{:S(2)}) collective-permute-start(bf16[2,10,3,16,96]{4,0,3,2,1:T(2,128)(2,1)S(1)} %get-tuple-element.55), channel_id=1, source_target_pairs={{0,2},{1,3},{4,6},{5,7},{8,10},{9,11},{12,14},{13,15},{16,18},{17,... | collective-permute-start | bytes 552968 | tf_op jit(solution)/shard_map/ppermute | solution.py:18
  26.1 2.6 collective-permute-done.2
  28.7 4.1 %collective-permute-done.3 = bf16[2,10,3,16,96]{4,0,3,2,1:T(2,128)(2,1)S(1)} collective-permute-done((bf16[2,10,3,16,96]{4,0,3,2,1:T(2,128)(2,1)S(1)}, bf16[2,10,3,16,96]{4,0,3,2,1:T(2,128)(2,1)S(1)}, u32[]{:S(2)}, u32[]{:S(2)}) %collective-permute-start.3) | collective-permute-done | bytes 184352 | tf_op jit(solution)/shard_map/ppermute | solution.py:21
  36.5 1.7 collective-permute-done.5
  38.2 7.8 %pad_maximum_fusion = bf16[2,10,14,22,96]{4,0,3,2,1:T(2,128)(2,1)S(1)} fusion(bf16[2,10,14,3,96]{4,0,3,2,1:T(2,128)(2,1)S(1)} %collective-permute-done.5, bf16[2,10,3,16,96]{4,0,3,2,1:T(2,128)(2,1)S(1)} %collective-permute-done.3, bf16[2,10,8,16,96]{4,0,3,2,1:T(2,128)(2,1)S(1)} %constant_dynamic-update-slice_fusion, ...), kind=kLoop, calls=%fused_computation.6 | loop fusion | flops 2365440 | bytes 2365440 | tf_op jit(solution)/shard_map/concatenate | solution.py:22
  46.0 19.1 %fusion.59 = (f32[2,4,8,16]{0,3,2,1:T(8,128)S(1)}, f32[2,4,8,16,96]{4,0,3,2,1:T(2,128)S(1)}) fusion(f32[96]{0:T(128)S(1)} %copy-done.12, bf16[2,10,14,22,96]{4,0,3,2,1:T(2,128)(2,1)S(1)} %pad_maximum_fusion, bf16[96,1,7,7,7]{0,4,3,2,1:T(8,128)(2,1)S(1)} %copy-done.9), kind=kOutput, calls=%fused_computation.92 | convolution fusion | flops 67632128 | bytes 1646272 | tf_op jit(solution)/shard_map/conv_general_dilated | solution.py:27
  70.1 16.3 %fusion = f32[1,7,7,7,96]{4,0,3,2,1:T(1,128)} fusion(bf16[2,10,14,22,96]{4,0,3,2,1:T(2,128)(2,1)} %copy-done.1, bf16[4,8,16,1,96]{4,2,1,0,3:T(8,128)(2,1)S(1)} %bitcast.90), kind=kOutput, calls=%fused_computation.2 | convolution fusion | flops 33718272 | bytes 1412736 | tf_op jit(solution)/shard_map/conv_general_dilated | solution.py:124
  87.3 3.6 %collective-permute-start.6 = (bf16[2,3,8,16,96]{4,0,3,2,1:T(2,128)(2,1)S(1)}, bf16[2,3,8,16,96]{4,0,3,2,1:T(2,128)(2,1)}, u32[]{:S(2)}, u32[]{:S(2)}) collective-permute-start(bf16[2,3,8,16,96]{4,0,3,2,1:T(2,128)(2,1)S(1)} %copy.121), channel_id=1, source_target_pairs={{0,4},{4,8},{8,12},{1,5},{5,9},{9,13},{2,6},{6,10},{10,14},{3,7},{... | collective-permute-start | bytes 442376 | tf_op jit(solution)/shard_map/ppermute | solution.py:18
  91.2 3.0 %collective-permute-start.7 = (bf16[2,3,8,16,96]{4,0,3,2,1:T(2,128)(2,1)S(1)}, bf16[2,3,8,16,96]{4,0,3,2,1:T(2,128)(2,1)}, u32[]{:S(2)}, u32[]{:S(2)}) collective-permute-start(bf16[2,3,8,16,96]{4,0,3,2,1:T(2,128)(2,1)S(1)} %copy.122), channel_id=1, source_target_pairs={{4,0},{8,4},{12,8},{5,1},{9,5},{13,9},{6,2},{10,6},{14,10},{7,3},{... | collective-permute-start | bytes 442376 | tf_op jit(solution)/shard_map/ppermute | solution.py:21
  94.2 15.4 %fusion.26 = f32[1,7,7,7,96]{4,0,3,2,1:T(1,128)} fusion(f32[1,7,7,7,96]{4,0,3,2,1:T(1,128)} %fusion, bf16[2,10,14,22,96]{4,0,3,2,1:T(2,128)(2,1)S(1)} %copy-done.2, bf16[4,8,16,1,96]{4,2,1,0,3:T(8,128)(2,1)} %bitcast.89), kind=kOutput, calls=%fused_computation.33 | convolution fusion | flops 33784128 | bytes 1544448 | tf_op jit(solution)/shard_map/conv_general_dilated | solution.py:124
  117.3 31.3 %all-reduce.6.cloned.1.call-done = f32[96,1,7,7,7]{0,4,3,2,1:T(8,128)} async-done(((f32[96,1,7,7,7]{0,4,3,2,1:T(8,128)}), f32[96,1,7,7,7]{0,4,3,2,1:T(8,128)}) %all-reduce.6.cloned.1.call-update) | async-done | bytes 131728 | tf_op jit(solution)/shard_map/psum | solution.py:135
  149.4 2.1 collective-permute-start.10
  152.9 7.5 %psum.58 = f32[96]{0:T(128)S(1)} all-reduce(f32[96]{0:T(128)S(1)} %broadcast_multiply_fusion.4), channel_id=1, replica_groups=mesh['groups'=2,'depth'=4,'rows'=2,'cols'=2] {'rows','cols'}, use_global_device_ids=true, to_apply=%region_7.0 | all-reduce | flops 96 | bytes 768 | tf_op jit(solution)/shard_map/psum | solution.py:135
  160.4 9.4 %psum.59 = f32[96]{0:T(128)} all-reduce(f32[96]{0:T(128)S(1)} %psum.58), channel_id=1, replica_groups=mesh['groups'=2,'depth'=4,'rows'=2,'cols'=2] {'depth'}, use_global_device_ids=true, to_apply=%region_8.0 | all-reduce | flops 96 | bytes 768 | tf_op jit(solution)/shard_map/psum | solution.py:135
  169.9 25.0 %all-reduce = (f32[192]{0:T(256)}, f32[384]{0:T(512)}) all-reduce(f32[192]{0:T(256)S(1)} %maximum_multiply_fusion, f32[384]{0:T(512)S(1)} %broadcast_multiply_fusion.3), channel_id=1, replica_groups=mesh['groups'=2,'depth'=4,'rows'=2,'cols'=2] {'depth','rows','cols'}, use_global_device_ids=true, to_apply=%region_11.0 | all-reduce | flops 576 | bytes 4608 | tf_op jit(solution)/shard_map/psum | solution.py:113
  194.9 1.8 copy.102
  196.7 7.8 %fusion.81 = bf16[2,10,14,22,96]{4,0,3,2,1:T(2,128)(2,1)S(1)} fusion(bf16[2,10,14,3,96]{4,0,3,2,1:T(2,128)(2,1)S(1)} %collective-permute-done.11, bf16[2,10,3,16,96]{4,0,3,2,1:T(2,128)(2,1)S(1)} %collective-permute-done.9, bf16[2,10,8,16,96]{4,0,3,2,1:T(2,128)(2,1)S(1)} %constant_dynamic-update-slice_fusion.3, ...), kind=kLoop, calls=%fused_computation.8.clone.1 | loop fusion | flops 2365440 | bytes 2365440 | tf_op jit(solution)/shard_map/conv_general_dilated | solution.py:27
  204.5 21.1 %fusion.4 = f32[2,4,8,16,96]{4,0,3,2,1:T(2,128)S(1)} fusion(bf16[96,1,7,7,7]{0,4,3,2,1:T(8,128)(2,1)S(1)} %copy-done.10, bf16[2,10,14,22,96]{4,0,3,2,1:T(2,128)(2,1)S(1)} %fusion.81), kind=kOutput, calls=%fused_computation.7 | convolution fusion | flops 67436544 | bytes 1641792 | tf_op jit(solution)/shard_map/conv_general_dilated | solution.py:27
  226.6 56.0 %all-reduce.10.cloned.1.call-done = (f32[96,384]{1,0:T(8,128)}, f32[384,96]{0,1:T(8,128)}) async-done(((f32[96,384]{1,0:T(8,128)}, f32[384,96]{0,1:T(8,128)}), (f32[96,384]{1,0:T(8,128)}, f32[384,96]{0,1:T(8,128)})) %all-reduce.10.cloned.1.call-update) | async-done | bytes 294928 | tf_op jit(solution)/shard_map/psum | solution.py:113
  282.6 1.6 copy.137
  (95 shorter events, 26.6 us)
Async XLA Ops:
  7.2 18.8 %copy-start = (bf16[768,192]{0,1:T(8,128)(2,1)S(1)}, bf16[768,192]{0,1:T(8,128)(2,1)}, u32[]{:S(2)}) copy-start(bf16[768,192]{0,1:T(8,128)(2,1)} %param.15) | copy-start | bytes 884740
  7.2 7.6 %copy-start.3 = (bf16[2,4,8,1536]{3,2,1,0:T(8,128)(2,1)S(1)}, bf16[2,4,8,1536]{3,2,1,0:T(8,128)(2,1)}, u32[]{:S(2)}) copy-start(bf16[2,4,8,1536]{3,2,1,0:T(8,128)(2,1)} %param.11) | copy-start | bytes 589828
  7.2 8.1 %copy-start.6 = (bf16[768]{0:T(1024)(128)(2,1)S(1)}, bf16[768]{0:T(1024)(128)(2,1)}, u32[]{:S(2)}) copy-start(bf16[768]{0:T(1024)(128)(2,1)} %param.12) | copy-start | bytes 4612
  7.2 141.4 %all-reduce.6.cloned.1.call-start = ((), (), s32[]{:S(2)}) async-start(), calls=%async_computation | async-start | bytes 401408 | tf_op jit(solution)/shard_map/psum | solution.py:135
  8.7 8.5 %collective-permute-start = (bf16[2,3,8,16,96]{4,0,3,2,1:T(2,128)(2,1)S(1)}, bf16[2,3,8,16,96]{4,0,3,2,1:T(2,128)(2,1)S(1)}, u32[]{:S(2)}, u32[]{:S(2)}) collective-permute-start(bf16[2,3,8,16,96]{4,0,3,2,1:T(2,128)(2,1)S(1)} %copy.119), channel_id=1, source_target_pairs={{0,4},{4,8},{8,12},{1,5},{5,9},{9,13},{2,6},{6,10},{10,14},{3,7},{... | collective-permute-start | bytes 442376 | tf_op jit(solution)/shard_map/ppermute | solution.py:18
  12.5 8.3 %collective-permute-start.1 = (bf16[2,3,8,16,96]{4,0,3,2,1:T(2,128)(2,1)S(1)}, bf16[2,3,8,16,96]{4,0,3,2,1:T(2,128)(2,1)S(1)}, u32[]{:S(2)}, u32[]{:S(2)}) collective-permute-start(bf16[2,3,8,16,96]{4,0,3,2,1:T(2,128)(2,1)S(1)} %copy.120), channel_id=1, source_target_pairs={{4,0},{8,4},{12,8},{5,1},{9,5},{13,9},{6,2},{10,6},{14,10},{7,3},{... | collective-permute-start | bytes 442376 | tf_op jit(solution)/shard_map/ppermute | solution.py:21
  15.1 11.0 %copy-start.8 = (f32[192]{0:T(256)S(1)}, f32[192]{0:T(256)}, u32[]{:S(2)}) copy-start(f32[192]{0:T(256)} %param.16) | copy-start | bytes 2308
  21.2 7.5 %collective-permute-start.2 = (bf16[2,10,3,16,96]{4,0,3,2,1:T(2,128)(2,1)S(1)}, bf16[2,10,3,16,96]{4,0,3,2,1:T(2,128)(2,1)S(1)}, u32[]{:S(2)}, u32[]{:S(2)}) collective-permute-start(bf16[2,10,3,16,96]{4,0,3,2,1:T(2,128)(2,1)S(1)} %get-tuple-element.55), channel_id=1, source_target_pairs={{0,2},{1,3},{4,6},{5,7},{8,10},{9,11},{12,14},{13,15},{16,18},{17,... | collective-permute-start | bytes 552968 | tf_op jit(solution)/shard_map/ppermute | solution.py:18
  24.6 8.2 %collective-permute-start.3 = (bf16[2,10,3,16,96]{4,0,3,2,1:T(2,128)(2,1)S(1)}, bf16[2,10,3,16,96]{4,0,3,2,1:T(2,128)(2,1)S(1)}, u32[]{:S(2)}, u32[]{:S(2)}) collective-permute-start(bf16[2,10,3,16,96]{4,0,3,2,1:T(2,128)(2,1)S(1)} %get-tuple-element.56), channel_id=1, source_target_pairs={{2,0},{3,1},{6,4},{7,5},{10,8},{11,9},{14,12},{15,13},{18,16},{19,... | collective-permute-start | bytes 552968 | tf_op jit(solution)/shard_map/ppermute | solution.py:21
  33.5 2.9 %collective-permute-start.4 = (bf16[2,10,14,3,96]{4,0,3,2,1:T(2,128)(2,1)S(1)}, bf16[2,10,14,3,96]{4,0,3,2,1:T(2,128)(2,1)S(1)}, u32[]{:S(2)}, u32[]{:S(2)}) collective-permute-start(bf16[2,10,14,3,96]{4,0,3,2,1:T(2,128)(2,1)S(1)} %get-tuple-element.51), channel_id=1, source_target_pairs={{0,1},{2,3},{4,5},{6,7},{8,9},{10,11},{12,13},{14,15},{16,17},{18,... | collective-permute-start | bytes 483848 | tf_op jit(solution)/shard_map/ppermute | solution.py:18
  34.8 3.4 %collective-permute-start.5 = (bf16[2,10,14,3,96]{4,0,3,2,1:T(2,128)(2,1)S(1)}, bf16[2,10,14,3,96]{4,0,3,2,1:T(2,128)(2,1)S(1)}, u32[]{:S(2)}, u32[]{:S(2)}) collective-permute-start(bf16[2,10,14,3,96]{4,0,3,2,1:T(2,128)(2,1)S(1)} %get-tuple-element.52), channel_id=1, source_target_pairs={{1,0},{3,2},{5,4},{7,6},{9,8},{11,10},{13,12},{15,14},{17,16},{19,... | collective-permute-start | bytes 483848 | tf_op jit(solution)/shard_map/ppermute | solution.py:21
  36.5 9.5 %copy-start.9 = (bf16[96,1,7,7,7]{0,4,3,2,1:T(8,128)(2,1)S(1)}, bf16[96,1,7,7,7]{0,4,3,2,1:T(8,128)(2,1)}, u32[]{:S(2)}) copy-start(bf16[96,1,7,7,7]{0,4,3,2,1:T(8,128)(2,1)} %param.13) | copy-start | bytes 197572
  36.5 9.5 %copy-start.12 = (f32[96]{0:T(128)S(1)}, f32[96]{0:T(128)}, u32[]{:S(2)}) copy-start(f32[96]{0:T(128)} %param.14) | copy-start | bytes 1156
  46.0 19.1 %copy-start.1 = (bf16[2,10,14,22,96]{4,0,3,2,1:T(2,128)(2,1)}, bf16[2,10,14,22,96]{4,0,3,2,1:T(2,128)(2,1)S(1)}, u32[]{:S(2)}) copy-start(bf16[2,10,14,22,96]{4,0,3,2,1:T(2,128)(2,1)S(1)} %pad_maximum_fusion) | copy-start | bytes 3548164
  87.1 7.1 %copy-start.2 = (bf16[2,10,14,22,96]{4,0,3,2,1:T(2,128)(2,1)S(1)}, bf16[2,10,14,22,96]{4,0,3,2,1:T(2,128)(2,1)}, u32[]{:S(2)}) copy-start(bf16[2,10,14,22,96]{4,0,3,2,1:T(2,128)(2,1)} %copy-done.1) | copy-start | bytes 3548164
  87.3 23.3 %collective-permute-start.6 = (bf16[2,3,8,16,96]{4,0,3,2,1:T(2,128)(2,1)S(1)}, bf16[2,3,8,16,96]{4,0,3,2,1:T(2,128)(2,1)}, u32[]{:S(2)}, u32[]{:S(2)}) collective-permute-start(bf16[2,3,8,16,96]{4,0,3,2,1:T(2,128)(2,1)S(1)} %copy.121), channel_id=1, source_target_pairs={{0,4},{4,8},{8,12},{1,5},{5,9},{9,13},{2,6},{6,10},{10,14},{3,7},{... | collective-permute-start | bytes 442376 | tf_op jit(solution)/shard_map/ppermute | solution.py:18
  91.2 20.9 %collective-permute-start.7 = (bf16[2,3,8,16,96]{4,0,3,2,1:T(2,128)(2,1)S(1)}, bf16[2,3,8,16,96]{4,0,3,2,1:T(2,128)(2,1)}, u32[]{:S(2)}, u32[]{:S(2)}) collective-permute-start(bf16[2,3,8,16,96]{4,0,3,2,1:T(2,128)(2,1)S(1)} %copy.122), channel_id=1, source_target_pairs={{4,0},{8,4},{12,8},{5,1},{9,5},{13,9},{6,2},{10,6},{14,10},{7,3},{... | collective-permute-start | bytes 442376 | tf_op jit(solution)/shard_map/ppermute | solution.py:21
  113.5 35.1 %collective-permute-start.8 = (bf16[2,10,3,16,96]{4,0,3,2,1:T(2,128)(2,1)S(1)}, bf16[2,10,3,16,96]{4,0,3,2,1:T(2,128)(2,1)S(1)}, u32[]{:S(2)}, u32[]{:S(2)}) collective-permute-start(bf16[2,10,3,16,96]{4,0,3,2,1:T(2,128)(2,1)S(1)} %get-tuple-element.53), channel_id=1, source_target_pairs={{0,2},{1,3},{4,6},{5,7},{8,10},{9,11},{12,14},{13,15},{16,18},{17,... | collective-permute-start | bytes 552968 | tf_op jit(solution)/shard_map/ppermute | solution.py:18
  115.0 33.7 %collective-permute-start.9 = (bf16[2,10,3,16,96]{4,0,3,2,1:T(2,128)(2,1)S(1)}, bf16[2,10,3,16,96]{4,0,3,2,1:T(2,128)(2,1)S(1)}, u32[]{:S(2)}, u32[]{:S(2)}) collective-permute-start(bf16[2,10,3,16,96]{4,0,3,2,1:T(2,128)(2,1)S(1)} %get-tuple-element.54), channel_id=1, source_target_pairs={{2,0},{3,1},{6,4},{7,5},{10,8},{11,9},{14,12},{15,13},{18,16},{19,... | collective-permute-start | bytes 552968 | tf_op jit(solution)/shard_map/ppermute | solution.py:21
  117.0 77.9 %all-reduce.8.cloned.1.call-start = ((), (), s32[]{:S(2)}) async-start(), calls=%async_computation.1 | async-start | bytes 401408 | tf_op jit(solution)/shard_map/psum | solution.py:135
  148.6 134.0 %all-reduce.10.cloned.1.call-start = ((), (), s32[]{:S(2)}) async-start(), calls=%async_computation.2 | async-start | bytes 589824 | tf_op jit(solution)/shard_map/psum | solution.py:113
  149.4 47.3 %collective-permute-start.10 = (bf16[2,10,14,3,96]{4,0,3,2,1:T(2,128)(2,1)S(1)}, bf16[2,10,14,3,96]{4,0,3,2,1:T(2,128)(2,1)S(1)}, u32[]{:S(2)}, u32[]{:S(2)}) collective-permute-start(bf16[2,10,14,3,96]{4,0,3,2,1:T(2,128)(2,1)S(1)} %get-tuple-element.49), channel_id=1, source_target_pairs={{0,1},{2,3},{4,5},{6,7},{8,9},{10,11},{12,13},{14,15},{16,17},{18,... | collective-permute-start | bytes 483848 | tf_op jit(solution)/shard_map/ppermute | solution.py:18
  151.5 45.2 %collective-permute-start.11 = (bf16[2,10,14,3,96]{4,0,3,2,1:T(2,128)(2,1)S(1)}, bf16[2,10,14,3,96]{4,0,3,2,1:T(2,128)(2,1)S(1)}, u32[]{:S(2)}, u32[]{:S(2)}) collective-permute-start(bf16[2,10,14,3,96]{4,0,3,2,1:T(2,128)(2,1)S(1)} %get-tuple-element.50), channel_id=1, source_target_pairs={{1,0},{3,2},{5,4},{7,6},{9,8},{11,10},{13,12},{15,14},{17,16},{19,... | collective-permute-start | bytes 483848 | tf_op jit(solution)/shard_map/ppermute | solution.py:21
  196.7 7.8 %copy-start.10 = (bf16[96,1,7,7,7]{0,4,3,2,1:T(8,128)(2,1)S(1)}, bf16[96,1,7,7,7]{0,4,3,2,1:T(8,128)(2,1)}, u32[]{:S(2)}) copy-start(bf16[96,1,7,7,7]{0,4,3,2,1:T(8,128)(2,1)} %param.13) | copy-start | bytes 197572
  (4 other events, 8.8 us)
Sparse Core Ops, SparseCore 0:
  117.1 31.3 all-reduce.5
  150.9 36.6 all-reduce.7
  191.6 90.8 all-reduce.9
